TPU v7x, 128 devices: a whole 4x4x4 slice. The times are simulated.
128 devices in a mesh: chi: 2 (over core), phi: 64 (over z, y, x).
Axes of the slice: x: 4, y: 4, z: 4, core: 2. Of those that a mesh axis runs over, the one named last changes fastest.
Arguments:
- frames: bfloat16 [1024, 8, 8, 2048], P('phi', 'chi'), may hold values from 0.25 to 8
- drift_rows: int32 [1024, 8], P('phi', 'chi'), may hold values from -2 to 2
- drift_cols: int32 [1024, 8], P('phi', 'chi'), may hold values from -24 to 24
- weight_index: int32 [1024, 8], P('phi', 'chi'), may hold values from 0 to 63
- blur_band: int32 [16384], P('chi'), may hold values from 0 to 3
Outputs:
- restored: float32 [1024, 8, 16384], P('phi', None, 'chi')
All inputs are finite; a program needn't handle non-finite values.
Results may differ from a plain program's by a relative error of at most 0.0003.
Values sent between devices are 32-bit elements; how exact they have to be, the bound alone decides.
A program may use at most 128 MiB of HBM per device.

v0:
```python
import jax
import jax.numpy as jnp
from jax import lax
from jax.sharding import PartitionSpec as P

ITERS = 3


def shifted(shard, axis, by):
    length = lax.axis_size(axis)
    pairs = [(i, i + by) for i in range(length) if 0 <= i + by < length]
    return lax.ppermute(shard, axis, pairs)


def shift_one(frame, row_drift, col_drift, table_index):
    padded = jnp.pad(frame.astype(jnp.float32), ((3, 3), (25, 25)))
    frac_y = (table_index // 8).astype(jnp.float32) / 8.0
    frac_x = (table_index % 8).astype(jnp.float32) / 8.0
    summed = jnp.zeros(frame.shape, jnp.float32)
    for a in range(2):
        for b in range(2):
            factor = (frac_y if a else 1.0 - frac_y) * (frac_x if b else 1.0 - frac_x)
            start_row = 3 - row_drift - a
            start_col = 25 - col_drift - b
            window = lax.dynamic_slice(padded, (start_row, start_col), frame.shape)
            summed = summed + factor * window
    return summed.reshape(-1)


def tap_weights(band_index):
    spread = 0.8 + 0.6 * band_index.astype(jnp.float32)
    offsets = jnp.arange(-4, 5).astype(jnp.float32)
    unnormed = jnp.exp(-offsets[:, None] ** 2 / (2.0 * spread[None, :] ** 2))
    return unnormed / jnp.sum(unnormed, axis=0, keepdims=True)


def phi_blur(field, weights):
    number = field.shape[1]
    padded = jnp.pad(field, ((0, 0), (4, 4), (0, 0)))
    phi_sum = jnp.zeros(field.shape, jnp.float32)
    for k in range(9):
        phi_sum = phi_sum + weights[k][None, None, :] * padded[:, k : k + number, :]
    return phi_sum


def chi_mix(own, below, above):
    before = jnp.concatenate([below, own[:-1]], axis=0)
    after = jnp.concatenate([own[1:], above], axis=0)
    return 0.25 * before + 0.5 * own + 0.25 * after


def body(frames, drift_rows, drift_cols, weight_index, blur_band):
    corrected = jax.vmap(jax.vmap(shift_one))(frames, drift_rows, drift_cols, weight_index)
    pixel_tiles = lax.all_to_all(corrected, "chi", split_axis=2, concat_axis=1, tiled=True)
    weights = tap_weights(blur_band)
    estimate = pixel_tiles + 0.1
    for iteration in range(ITERS):
        summed = phi_blur(estimate, weights)
        below = shifted(summed[-1:], "phi", 1)
        above = shifted(summed[:1], "phi", -1)
        blurred = chi_mix(summed, below, above)
        ratio = pixel_tiles / (blurred + 0.1)
        ratio_sum = phi_blur(ratio, weights)
        ratio_below = shifted(ratio_sum[-1:], "phi", 1)
        ratio_above = shifted(ratio_sum[:1], "phi", -1)
        estimate = estimate * chi_mix(ratio_sum, ratio_below, ratio_above)
    return estimate


def solution(mesh):
    return jax.shard_map(
        body,
        mesh=mesh,
        in_specs=(
            P("phi", "chi", None, None),
            P("phi", "chi"),
            P("phi", "chi"),
            P("phi", "chi"),
            P("chi"),
        ),
        out_specs=P("phi", None, "chi"),
        check_vma=False,
    )
```

profile of v0, /device:TPU:30, one launch (start us, length us, event | category | flops | bytes accessed | tf_op | source)
XLA Modules:
  0.0 1755.4 jit_solution(11334240100492443829)
XLA Ops:
  0.9 8.4 pad_convert_fusion
  11.9 306.2 %while.4 = (s32[]{:T(128)}, f32[16,4,14,2098]{3,2,1,0:T(8,128)}, s32[64,4]{0,1:T(4,128)S(1)}, f32[64,8,2048]{2,1,0:T(8,128)}, s32[]{:T(128)}) while((s32[]{:T(128)}, f32[16,4,14,2098]{3,2,1,0:T(8,128)}, s32[64,4]{0,1:T(4,128)S(1)}, f32[64,8,2048]{2,1,0:T(8,128)}, s32[]{:T(128)}) %tuple.108), condition=%wide.while_cond, body=%wide.while_body.sunk | while | flops 2 | bytes 133761 | solution.py:25
  318.0 6.1 gather.21
  326.8 306.4 %while.5 = (s32[]{:T(128)}, f32[16,4,14,2098]{3,2,1,0:T(8,128)}, s32[64,4]{0,1:T(4,128)S(1)}, f32[64,8,2048]{2,1,0:T(8,128)}, s32[]{:T(128)}) while((s32[]{:T(128)}, f32[16,4,14,2098]{3,2,1,0:T(8,128)}, s32[64,4]{0,1:T(4,128)S(1)}, f32[64,8,2048]{2,1,0:T(8,128)}, s32[]{:T(128)}) %tuple.111), condition=%wide.while_cond.1, body=%wide.while_body.1.sunk | while | flops 2 | bytes 133761 | solution.py:25
  633.2 6.0 gather.23
  642.0 306.8 %while.6 = (s32[]{:T(128)}, f32[16,4,14,2098]{3,2,1,0:T(8,128)}, s32[64,4]{0,1:T(4,128)S(1)}, f32[64,8,2048]{2,1,0:T(8,128)}, s32[]{:T(128)}) while((s32[]{:T(128)}, f32[16,4,14,2098]{3,2,1,0:T(8,128)}, s32[64,4]{0,1:T(4,128)S(1)}, f32[64,8,2048]{2,1,0:T(8,128)}, s32[]{:T(128)}) %tuple.112), condition=%wide.while_cond.2, body=%wide.while_body.2.sunk | while | flops 2 | bytes 133761 | solution.py:25
  666.6 4.1 bitcast_dynamic-update-slice_fusion.10
  671.4 4.1 bitcast_dynamic-update-slice_fusion.10
  676.2 4.1 bitcast_dynamic-update-slice_fusion.10
  681.0 4.1 bitcast_dynamic-update-slice_fusion.10
  714.5 4.1 bitcast_dynamic-update-slice_fusion.10
  719.3 4.1 bitcast_dynamic-update-slice_fusion.10
  724.1 4.1 bitcast_dynamic-update-slice_fusion.10
  728.9 4.1 bitcast_dynamic-update-slice_fusion.10
  757.7 4.1 bitcast_dynamic-update-slice_fusion.10
  762.5 4.1 bitcast_dynamic-update-slice_fusion.10
  767.2 4.1 bitcast_dynamic-update-slice_fusion.10
  772.0 4.1 bitcast_dynamic-update-slice_fusion.10
  805.6 4.1 bitcast_dynamic-update-slice_fusion.10
  810.4 4.1 bitcast_dynamic-update-slice_fusion.10
  815.2 4.1 bitcast_dynamic-update-slice_fusion.10
  820.0 4.1 bitcast_dynamic-update-slice_fusion.10
  848.7 4.1 bitcast_dynamic-update-slice_fusion.10
  853.5 4.1 bitcast_dynamic-update-slice_fusion.10
  858.3 4.1 bitcast_dynamic-update-slice_fusion.10
  863.1 4.1 bitcast_dynamic-update-slice_fusion.10
  896.7 4.1 bitcast_dynamic-update-slice_fusion.10
  901.5 4.1 bitcast_dynamic-update-slice_fusion.10
  906.2 4.1 bitcast_dynamic-update-slice_fusion.10
  911.0 4.1 bitcast_dynamic-update-slice_fusion.10
  939.8 4.1 bitcast_dynamic-update-slice_fusion.10
  944.6 4.1 bitcast_dynamic-update-slice_fusion.10
  948.7 6.0 gather.25
  957.5 303.8 %while.7 = (s32[]{:T(128)}, f32[16,4,14,2098]{3,2,1,0:T(8,128)}, s32[64,4]{0,1:T(4,128)S(1)}, f32[64,8,2048]{2,1,0:T(8,128)}, s32[]{:T(128)}) while((s32[]{:T(128)}, f32[16,4,14,2098]{3,2,1,0:T(8,128)}, s32[64,4]{0,1:T(4,128)S(1)}, f32[64,8,2048]{2,1,0:T(8,128)}, s32[]{:T(128)}) %tuple.113), condition=%wide.while_cond.3, body=%wide.while_body.3.sunk | while | flops 2 | bytes 133761 | solution.py:25
  1261.3 6.0 gather.27
  1267.7 8.6 multiply_add_fusion
  1276.3 23.6 %copy.59 = f32[16,4,16384]{0,1,2:T(4,128)} copy(f32[16,4,16384]{2,1,0:T(4,128)} %multiply_add_fusion) | data formatting | bytes 8388608 | tf_op jit(solution)/shard_map/vmap(vmap())/add | solution.py:26
  1299.9 42.6 %reshape.139 = f32[2,1,524288]{2,1,0:T(1,128)} reshape(f32[16384,4,16]{2,1,0:T(4,128)} %bitcast.94) | data formatting | bytes 8388608
  1342.5 5.6 all-to-all-start
  1348.1 4.5 all-to-all-done
  1353.1 16.7 reduce
  1369.8 44.6 %reshape.140 = f32[16384,4,16]{2,1,0:T(4,128)} reshape(f32[2,524288]{1,0:T(2,128)} %reduce) | data formatting | bytes 8388608
  1414.5 25.1 %copy.60 = f32[16,2,4,8192]{3,2,1,0:T(4,128)} copy(f32[16,2,4,8192]{0,2,3,1:T(4,128)} %bitcast.95) | data formatting | bytes 8388608 | tf_op jit(solution)/shard_map/all_to_all | solution.py:54
  1439.5 5.3 all_to_all.16
  1448.0 4.7 fusion.8
  1463.0 7.3 collective-permute-done.1
  1470.3 21.8 %fusion.99 = f32[16,8,8192]{2,1,0:T(8,128)} fusion(f32[16,8,8192]{2,1,0:T(8,128)} %all_to_all.16, f32[15,8,8192]{2,1,0:T(8,128)} %get-tuple-element.108, f32[1,8,8192]{2,1,0:T(8,128)S(1)} %collective-permute-done, f32[1,8,8192]{2,1,0:T(8,128)S(1)} %collective-permute-done.1, f32[15,8,8192]{2,1,0:T(8,128)} %get-tuple-element.107, f32[8192]{0:T(1024)S(1)} %bitcast.109, ...), kind=kLoop, calls=%fused_computation.157 | loop fusion | flops 27262976 | bytes 21266432 | tf_op jit(solution)/shard_map/div | solution.py:62
  1492.2 16.1 fusion.24
  1518.3 5.3 collective-permute-done.3
  1523.6 21.3 %fusion.102 = f32[16,8,8192]{2,1,0:T(8,128)} fusion(f32[15,8,8192]{2,1,0:T(8,128)} %get-tuple-element.104, f32[1,8,8192]{2,1,0:T(8,128)S(1)} %collective-permute-done.2, f32[1,8,8192]{2,1,0:T(8,128)S(1)} %collective-permute-done.3, f32[15,8,8192]{2,1,0:T(8,128)} %get-tuple-element.103, f32[16,8,8192]{2,1,0:T(8,128)} %all_to_all.16, f32[8192]{0:T(1024)S(1)} %bitcast.111, ...), kind=kLoop, calls=%fused_computation.162 | loop fusion | flops 27262976 | bytes 21266432 | tf_op jit(solution)/shard_map/mul | solution.py:66
  1544.9 16.6 fusion.40
  1571.6 4.4 collective-permute-done.5
  1576.0 21.8 %fusion.106 = f32[16,8,8192]{2,1,0:T(8,128)} fusion(f32[16,8,8192]{2,1,0:T(8,128)} %all_to_all.16, f32[15,8,8192]{2,1,0:T(8,128)} %get-tuple-element.100, f32[1,8,8192]{2,1,0:T(8,128)S(1)} %collective-permute-done.4, f32[1,8,8192]{2,1,0:T(8,128)S(1)} %collective-permute-done.5, f32[15,8,8192]{2,1,0:T(8,128)} %get-tuple-element.99, f32[8192]{0:T(1024)S(1)} %bitcast.113, ...), kind=kLoop, calls=%fused_computation.168 | loop fusion | flops 27262976 | bytes 21266432 | tf_op jit(solution)/shard_map/div | solution.py:62
  1597.8 16.1 fusion.56
  1615.9 4.2 collective-permute-start.7
  1624.1 4.4 collective-permute-done.7
  1628.4 21.3 %fusion.109 = f32[16,8,8192]{2,1,0:T(8,128)} fusion(f32[16,8,8192]{2,1,0:T(8,128)} %fusion.102, f32[15,8,8192]{2,1,0:T(8,128)} %get-tuple-element.96, f32[1,8,8192]{2,1,0:T(8,128)S(1)} %collective-permute-done.6, f32[1,8,8192]{2,1,0:T(8,128)S(1)} %collective-permute-done.7, f32[15,8,8192]{2,1,0:T(8,128)} %get-tuple-element.95, f32[8192]{0:T(1024)S(1)} %bitcast.115, ...), kind=kLoop, calls=%fused_computation.173 | loop fusion | flops 26214400 | bytes 21266432 | tf_op jit(solution)/shard_map/mul | solution.py:66
  1649.7 16.6 fusion.72
  1668.3 4.2 collective-permute-start.9
  1676.6 4.3 collective-permute-done.9
  1680.8 21.8 %fusion.113 = f32[16,8,8192]{2,1,0:T(8,128)} fusion(f32[16,8,8192]{2,1,0:T(8,128)} %all_to_all.16, f32[15,8,8192]{2,1,0:T(8,128)} %get-tuple-element.92, f32[1,8,8192]{2,1,0:T(8,128)S(1)} %collective-permute-done.8, f32[1,8,8192]{2,1,0:T(8,128)S(1)} %collective-permute-done.9, f32[15,8,8192]{2,1,0:T(8,128)} %get-tuple-element.91, f32[8192]{0:T(1024)S(1)} %bitcast.117, ...), kind=kLoop, calls=%fused_computation.179 | loop fusion | flops 27262976 | bytes 21266432 | tf_op jit(solution)/shard_map/div | solution.py:62
  1702.6 16.3 fusion.88
  1728.9 4.5 collective-permute-done.11
  1733.4 21.5 %fusion.116 = f32[16,8,8192]{2,1,0:T(8,128)} fusion(f32[16,8,8192]{2,1,0:T(8,128)} %fusion.109, f32[15,8,8192]{2,1,0:T(8,128)} %get-tuple-element.88, f32[1,8,8192]{2,1,0:T(8,128)S(1)} %collective-permute-done.10, f32[1,8,8192]{2,1,0:T(8,128)S(1)} %collective-permute-done.11, f32[15,8,8192]{2,1,0:T(8,128)} %get-tuple-element.87, f32[8192]{0:T(1024)S(1)} %bitcast.119, ...), kind=kLoop, calls=%fused_computation.184 | loop fusion | flops 26214400 | bytes 21266432 | tf_op jit(solution)/shard_map/mul | solution.py:66
  (805 shorter events, 1182.9 us)
Async XLA Ops:
  1261.3 6.0 copy-start.2
  1342.5 10.1 all-to-all-start
  1444.8 2.6 copy-start.1
  1447.4 5.3 copy-start
  1452.8 10.2 collective-permute-start
  1456.2 14.2 collective-permute-start.1
  1508.4 10.0 collective-permute-start.2
  1510.3 13.3 collective-permute-start.3
  1561.6 10.0 collective-permute-start.4
  1563.5 12.5 collective-permute-start.5
  1614.0 10.1 collective-permute-start.6
  1615.9 12.5 collective-permute-start.7
  1666.4 10.2 collective-permute-start.8
  1668.3 12.5 collective-permute-start.9
  1719.0 9.9 collective-permute-start.10
  1720.9 12.5 collective-permute-start.11
where the time goes:
time: 1780 us; the launch traced here: 1760 us
  local copies, waits for them, and re-layouts  1420 us (80%)
  other arithmetic  254 us (14%)
  starting transfers between devices  41.6 us (2%)
  waiting for transfers between devices  35.1 us (2%)
    gather x768, local copies, waits for them, and re-layouts  1220 us
    unnamed x14, local copies, waits for them, and re-layouts  97.3 us
    add x6, other arithmetic, phi_blur(): phi_sum = phi_sum + weights[k][None, None, :] * padded[:, k:k + number, :]  86.5 us
    div x3, other arithmetic, body(): ratio = pixel_tiles / (blurred + 0.1)  65.5 us
    mul x3, other arithmetic, body(): estimate = estimate * chi_mix(ratio_sum, ratio_below, ratio_above)  64.1 us
    ppermute x12, starting transfers between devices, shifted(): return lax.ppermute(shard, axis, pairs)  36 us
  transfers between devices with their start and end apart: 13, of which 8 were waited for; matrix products, arithmetic and copies ran while one was open for 1% of the time, Pallas kernels for 0%

commit v1 on v0

--- a/solution.py
+++ b/solution.py
@@ -51,7 +51,10 @@
 
 def body(frames, drift_rows, drift_cols, weight_index, blur_band):
     corrected = jax.vmap(jax.vmap(shift_one))(frames, drift_rows, drift_cols, weight_index)
-    pixel_tiles = lax.all_to_all(corrected, "chi", split_axis=2, concat_axis=1, tiled=True)
+    pixel_tiles = jnp.concatenate(
+        lax.all_to_all(jnp.stack(jnp.split(corrected, lax.axis_size("chi"), axis=2)), "chi", 0, 0),
+        axis=1,
+    )
     weights = tap_weights(blur_band)
     estimate = pixel_tiles + 0.1
     for iteration in range(ITERS):

time: 1780 us -> 1610 us (0.904)
  local copies, waits for them, and re-layouts: 1420 us -> 1310 us
  other arithmetic: 254 us -> 191 us
    unnamed x14, local copies, waits for them, and re-layouts: 97.3 us -> 11.5 us
    all_to_all x3 -> x1, local copies, waits for them, and re-layouts: 30.9 us -> 4.62 us  [body(): lax.all_to_all(jnp.stack(jnp.split(corrected, lax.axis_size('chi'), axis=...]
    add x1 -> x0, local copies, waits for them, and re-layouts: 23.6 us -> none  [shift_one(): summed = summed + factor * window]
    add x6, other arithmetic: 86.5 us -> 63.9 us  [phi_blur(): phi_sum = phi_sum + weights[k][None, None, :] * padded[:, k:k + number, :]]
  transfers between devices with their start and end apart: 13 -> 13, of which waited for: 8 -> 8; matrix products, arithmetic and copies ran while one was open for 1% -> 2% of each run, Pallas kernels for 0% -> 0%
where the time goes in v1:
time: 1610 us; the launch traced here: 1580 us
  local copies, waits for them, and re-layouts  1310 us (81%)
  other arithmetic  191 us (12%)
  starting transfers between devices  41.6 us (3%)
  waiting for transfers between devices  34.3 us (2%)
    gather x768, local copies, waits for them, and re-layouts  1240 us
    add x6, other arithmetic, phi_blur(): phi_sum = phi_sum + weights[k][None, None, :] * padded[:, k:k + number, :]  63.9 us
    mul x3, other arithmetic, body(): estimate = estimate * chi_mix(ratio_sum, ratio_below, ratio_above)  53.4 us
    div x3, other arithmetic, body(): ratio = pixel_tiles / (blurred + 0.1)  52.7 us
    ppermute x12, starting transfers between devices, shifted(): return lax.ppermute(shard, axis, pairs)  35.8 us
  transfers between devices with their start and end apart: 13, of which 8 were waited for; matrix products, arithmetic and copies ran while one was open for 2% of the time, Pallas kernels for 0%

profile of v1, /device:TPU:30, one launch (start us, length us, event | category | flops | bytes accessed | tf_op | source)
XLA Modules:
  0.0 1582.2 jit_solution(16371779978393597203)
XLA Ops:
  0.9 8.4 pad_convert_fusion
  11.9 307.9 %while.4 = (s32[]{:T(128)}, f32[16,4,14,2098]{3,2,1,0:T(8,128)}, s32[64,4]{0,1:T(4,128)S(1)}, f32[64,8,2048]{2,1,0:T(8,128)}, s32[]{:T(128)}) while((s32[]{:T(128)}, f32[16,4,14,2098]{3,2,1,0:T(8,128)}, s32[64,4]{0,1:T(4,128)S(1)}, f32[64,8,2048]{2,1,0:T(8,128)}, s32[]{:T(128)}) %tuple.109), condition=%wide.while_cond, body=%wide.while_body.sunk | while | flops 2 | bytes 133761 | solution.py:25
  319.7 6.1 gather.21
  328.5 311.6 %while.5 = (s32[]{:T(128)}, f32[16,4,14,2098]{3,2,1,0:T(8,128)}, s32[64,4]{0,1:T(4,128)S(1)}, f32[64,8,2048]{2,1,0:T(8,128)}, s32[]{:T(128)}) while((s32[]{:T(128)}, f32[16,4,14,2098]{3,2,1,0:T(8,128)}, s32[64,4]{0,1:T(4,128)S(1)}, f32[64,8,2048]{2,1,0:T(8,128)}, s32[]{:T(128)}) %tuple.112), condition=%wide.while_cond.1, body=%wide.while_body.1.sunk | while | flops 2 | bytes 133761 | solution.py:25
  640.2 6.0 gather.23
  648.9 315.4 %while.6 = (s32[]{:T(128)}, f32[16,4,14,2098]{3,2,1,0:T(8,128)}, s32[64,4]{0,1:T(4,128)S(1)}, f32[64,8,2048]{2,1,0:T(8,128)}, s32[]{:T(128)}) while((s32[]{:T(128)}, f32[16,4,14,2098]{3,2,1,0:T(8,128)}, s32[64,4]{0,1:T(4,128)S(1)}, f32[64,8,2048]{2,1,0:T(8,128)}, s32[]{:T(128)}) %tuple.113), condition=%wide.while_cond.2, body=%wide.while_body.2.sunk | while | flops 2 | bytes 133761 | solution.py:25
  649.6 4.2 bitcast_dynamic-update-slice_fusion.10
  654.5 4.2 bitcast_dynamic-update-slice_fusion.10
  659.5 4.2 bitcast_dynamic-update-slice_fusion.10
  664.4 4.2 bitcast_dynamic-update-slice_fusion.10
  669.3 4.2 bitcast_dynamic-update-slice_fusion.10
  674.2 4.2 bitcast_dynamic-update-slice_fusion.10
  679.2 4.2 bitcast_dynamic-update-slice_fusion.10
  684.1 4.2 bitcast_dynamic-update-slice_fusion.10
  689.0 4.2 bitcast_dynamic-update-slice_fusion.10
  694.0 4.2 bitcast_dynamic-update-slice_fusion.10
  698.9 4.2 bitcast_dynamic-update-slice_fusion.10
  703.8 4.2 bitcast_dynamic-update-slice_fusion.10
  708.7 4.2 bitcast_dynamic-update-slice_fusion.10
  713.7 4.2 bitcast_dynamic-update-slice_fusion.10
  718.6 4.2 bitcast_dynamic-update-slice_fusion.10
  728.5 4.2 bitcast_dynamic-update-slice_fusion.10
  733.4 4.2 bitcast_dynamic-update-slice_fusion.10
  738.3 4.2 bitcast_dynamic-update-slice_fusion.10
  743.2 4.2 bitcast_dynamic-update-slice_fusion.10
  748.2 4.2 bitcast_dynamic-update-slice_fusion.10
  753.1 4.2 bitcast_dynamic-update-slice_fusion.10
  758.0 4.2 bitcast_dynamic-update-slice_fusion.10
  762.9 4.2 bitcast_dynamic-update-slice_fusion.10
  767.9 4.2 bitcast_dynamic-update-slice_fusion.10
  772.8 4.2 bitcast_dynamic-update-slice_fusion.10
  777.7 4.2 bitcast_dynamic-update-slice_fusion.10
  782.7 4.2 bitcast_dynamic-update-slice_fusion.10
  787.6 4.2 bitcast_dynamic-update-slice_fusion.10
  792.5 4.2 bitcast_dynamic-update-slice_fusion.10
  797.4 4.2 bitcast_dynamic-update-slice_fusion.10
  802.4 4.2 bitcast_dynamic-update-slice_fusion.10
  807.3 4.2 bitcast_dynamic-update-slice_fusion.10
  812.2 4.2 bitcast_dynamic-update-slice_fusion.10
  822.1 4.2 bitcast_dynamic-update-slice_fusion.10
  964.3 6.0 gather.25
  973.0 304.3 %while.7 = (s32[]{:T(128)}, f32[16,4,14,2098]{3,2,1,0:T(8,128)}, s32[64,4]{0,1:T(4,128)S(1)}, f32[64,8,2048]{2,1,0:T(8,128)}, s32[]{:T(128)}) while((s32[]{:T(128)}, f32[16,4,14,2098]{3,2,1,0:T(8,128)}, s32[64,4]{0,1:T(4,128)S(1)}, f32[64,8,2048]{2,1,0:T(8,128)}, s32[]{:T(128)}) %tuple.114), condition=%wide.while_cond.3, body=%wide.while_body.3.sunk | while | flops 2 | bytes 133761 | solution.py:25
  1277.3 6.1 gather.27
  1283.7 7.3 multiply_add_fusion
  1294.6 5.8 all-to-all-start
  1300.4 4.5 all-to-all-done
  1304.9 4.6 copy.46
  1326.3 7.3 collective-permute-done.1
  1333.7 17.4 %fusion.99 = f32[16,8,8192]{2,0,1:T(8,128)} fusion(f32[15,8,8192]{2,0,1:T(8,128)} %get-tuple-element.108, f32[1,8,8192]{2,0,1:T(1,128)S(1)} %collective-permute-done, f32[1,8,8192]{2,0,1:T(1,128)S(1)} %collective-permute-done.1, f32[15,8,8192]{2,0,1:T(8,128)} %get-tuple-element.107, f32[2,16,4,8192]{3,1,2,0:T(8,128)} %copy-done, f32[8192]{0:T(1024)S(1)} %bitcast.115, ...), kind=kLoop, calls=%fused_computation.158 | loop fusion | flops 27262976 | bytes 21266432 | tf_op jit(solution)/shard_map/div | solution.py:65
  1351.1 12.1 fusion.24
  1373.8 5.0 collective-permute-done.3
  1378.8 17.8 %fusion.102 = f32[16,8,8192]{2,0,1:T(8,128)} fusion(f32[15,8,8192]{2,0,1:T(8,128)} %get-tuple-element.104, f32[1,8,8192]{2,0,1:T(1,128)S(1)} %collective-permute-done.2, f32[1,8,8192]{2,0,1:T(1,128)S(1)} %collective-permute-done.3, f32[15,8,8192]{2,0,1:T(8,128)} %get-tuple-element.103, f32[2,16,4,8192]{3,1,2,0:T(8,128)} %copy-done, f32[8192]{0:T(1024)S(1)} %bitcast.117, ...), kind=kLoop, calls=%fused_computation.163 | loop fusion | flops 27262976 | bytes 21266432 | tf_op jit(solution)/shard_map/mul | solution.py:69
  1396.6 12.1 fusion.40
  1419.1 4.4 collective-permute-done.5
  1423.5 17.6 %fusion.106 = f32[16,8,8192]{2,0,1:T(8,128)} fusion(f32[15,8,8192]{2,0,1:T(8,128)} %get-tuple-element.100, f32[1,8,8192]{2,0,1:T(1,128)S(1)} %collective-permute-done.4, f32[1,8,8192]{2,0,1:T(1,128)S(1)} %collective-permute-done.5, f32[15,8,8192]{2,0,1:T(8,128)} %get-tuple-element.99, f32[2,16,4,8192]{3,1,2,0:T(8,128)} %copy-done, f32[8192]{0:T(1024)S(1)} %bitcast.119, ...), kind=kLoop, calls=%fused_computation.169 | loop fusion | flops 27262976 | bytes 21266432 | tf_op jit(solution)/shard_map/div | solution.py:65
  1441.1 12.1 fusion.56
  1455.5 4.3 collective-permute-start.7
  1468.0 17.8 %fusion.109 = f32[16,8,8192]{2,0,1:T(8,128)} fusion(f32[16,8,8192]{2,0,1:T(8,128)} %fusion.102, f32[15,8,8192]{2,0,1:T(8,128)} %get-tuple-element.96, f32[1,8,8192]{2,0,1:T(1,128)S(1)} %collective-permute-done.6, f32[1,8,8192]{2,0,1:T(1,128)S(1)} %collective-permute-done.7, f32[15,8,8192]{2,0,1:T(8,128)} %get-tuple-element.95, f32[8192]{0:T(1024)S(1)} %bitcast.121, ...), kind=kLoop, calls=%fused_computation.174 | loop fusion | flops 26214400 | bytes 21266432 | tf_op jit(solution)/shard_map/mul | solution.py:69
  1485.9 12.1 fusion.72
  1508.4 4.6 collective-permute-done.9
  1513.0 17.6 %fusion.113 = f32[16,8,8192]{2,0,1:T(8,128)} fusion(f32[15,8,8192]{2,0,1:T(8,128)} %get-tuple-element.92, f32[1,8,8192]{2,0,1:T(1,128)S(1)} %collective-permute-done.8, f32[1,8,8192]{2,0,1:T(1,128)S(1)} %collective-permute-done.9, f32[15,8,8192]{2,0,1:T(8,128)} %get-tuple-element.91, f32[2,16,4,8192]{3,1,2,0:T(8,128)} %copy-done, f32[8192]{0:T(1024)S(1)} %bitcast.123, ...), kind=kLoop, calls=%fused_computation.180 | loop fusion | flops 27262976 | bytes 21266432 | tf_op jit(solution)/shard_map/div | solution.py:65
  1530.6 12.1 fusion.88
  1557.5 17.8 %fusion.116 = f32[16,8,8192]{2,0,1:T(8,128)} fusion(f32[16,8,8192]{2,0,1:T(8,128)} %fusion.109, f32[15,8,8192]{2,0,1:T(8,128)} %get-tuple-element.88, f32[1,8,8192]{2,0,1:T(1,128)S(1)} %collective-permute-done.10, f32[1,8,8192]{2,0,1:T(1,128)S(1)} %collective-permute-done.11, f32[15,8,8192]{2,0,1:T(8,128)} %get-tuple-element.87, f32[8192]{0:T(1024)S(1)} %bitcast.125, ...), kind=kLoop, calls=%fused_computation.185 | loop fusion | flops 26214400 | bytes 21266432 | tf_op jit(solution)/shard_map/mul | solution.py:69
  1575.4 6.6 copy.47
  (804 shorter events, 1183.4 us)
Async XLA Ops:
  1277.3 6.1 copy-start.3
  1294.6 10.3 all-to-all-start
  1309.5 2.0 copy-start
  1309.5 2.0 copy-start.2
  1311.5 4.2 copy-start.1
  1316.1 10.2 collective-permute-start
  1319.5 14.2 collective-permute-start.1
  1363.6 10.2 collective-permute-start.2
  1365.5 13.3 collective-permute-start.3
  1409.1 10.0 collective-permute-start.4
  1411.0 12.5 collective-permute-start.5
  1453.6 10.4 collective-permute-start.6
  1455.5 12.5 collective-permute-start.7
  1498.3 10.0 collective-permute-start.8
  1500.5 12.5 collective-permute-start.9
  1543.1 10.2 collective-permute-start.10
  1545.1 12.5 collective-permute-start.11
